TPU v7x, 128 devices: a whole 4x4x4 slice. The times are simulated.
128 devices in a mesh: dp: 4 (over x), tensor: 32 (over y, z, core).
Axes of the slice: x: 4, y: 4, z: 4, core: 2. Of those that a mesh axis runs over, the one named last changes fastest.
Arguments:
- tokens: bfloat16 [16384, 2048], P(('dp', 'tensor')), may hold values from -6 to 6
- norm_gain: bfloat16 [2048], replicated, may hold values from 0.099609375 to 1.8984375
- routes: int32 [16384, 6], P(('dp', 'tensor')), may hold values from 0 to 31, all different within a row; in each aligned block of 128 rows (0 to 127, 128 to 255, ...) at most 32 rows name the same one
- route_gates: bfloat16 [16384, 6], P(('dp', 'tensor')), may hold values from 0.19921875 to 1
- lengths: int32 [24], replicated, may hold values from 1 to 1920, 16384 in all
- request_adapter: int32 [24], replicated, may hold values from 0 to 31
- adapter_slot: int32 [32], replicated, may hold values from 0 to 31, each once
- expert_gate: bfloat16 [32, 2048, 1408], P('tensor'), may hold values from -0.125 to 0.125
- expert_up: bfloat16 [32, 2048, 1408], P('tensor'), may hold values from -0.125 to 0.125
- expert_down: bfloat16 [32, 1408, 2048], P('tensor'), may hold values from -0.15625 to 0.15625
- shared_gate: bfloat16 [2048, 1408], P(None, 'dp'), may hold values from -0.125 to 0.125
- shared_up_weight: bfloat16 [2048, 1408], P(None, 'dp'), may hold values from -0.125 to 0.125
- shared_down: bfloat16 [1408, 2048], P('dp'), may hold values from -0.15625 to 0.15625
- adapter_down: bfloat16 [32, 2048, 16], P('dp'), may hold values from -0.125 to 0.125
- adapter_up: bfloat16 [32, 16, 2048], P('dp'), may hold values from -1.5 to 1.5
- head_weight: bfloat16 [2048, 65536], P(None, ('dp', 'tensor')), may hold values from -0.375 to 0.375
Outputs:
- sublayer_out: bfloat16 [16384, 2048], P(('dp', 'tensor'))
- last_norm: float32 [24], replicated
- block_logit: float32 [24, 32], P(None, 'tensor')
Inputs may be any that keep to these rules, and one draw needn't show every extreme that they name: `routes`: in each aligned block of 128 rows (the rows of one device), no expert is named by more than 32 rows, a bound that some block reaches. The lengths sum to 16384; the largest is exactly 1920. Each position of the store appears once: adapter a is stored at position adapter_slot[a] of adapter_down and adapter_up.
All inputs are finite; a program needn't handle non-finite values.
Results may differ from a plain program's by a relative error of at most 0.0066.
Values may be sent and summed in bfloat16 or wider, within the bound.
A program may use at most 128 MiB of HBM per device.

v0:
```python
import jax
import jax.numpy as jnp
from jax import lax
from jax.sharding import PartitionSpec as P

CAP = 32


def apply_norm(tokens, norm_gain):
    values = tokens.astype(jnp.float32)
    scaled = lax.rsqrt(jnp.mean(values * values, axis=-1, keepdims=True) + 1e-06)
    return (values * scaled * norm_gain.astype(jnp.float32)).astype(jnp.bfloat16)


def feed_forward(inputs, gate_mat, up_mat, down_mat):
    gate_portion = jnp.dot(inputs, gate_mat, preferred_element_type=jnp.float32)
    up_part = jnp.dot(inputs, up_mat, preferred_element_type=jnp.float32)
    hidden = (jax.nn.silu(gate_portion) * up_part).astype(jnp.bfloat16)
    return jnp.dot(hidden, down_mat, preferred_element_type=jnp.float32)


def token_slots(positions, lengths, request_adapter, adapter_slot):
    request_ends = jnp.cumsum(lengths)
    request = jnp.sum((request_ends[None, :] <= positions[:, None]).astype(jnp.int32), axis=1)
    request_pick = (
        request[:, None] == jnp.arange(request_adapter.shape[0], dtype=jnp.int32)[None, :]
    )
    adapter = jnp.sum(jnp.where(request_pick, request_adapter[None, :], 0), axis=1)
    adapter_pick = adapter[:, None] == jnp.arange(adapter_slot.shape[0], dtype=jnp.int32)[None, :]
    return jnp.sum(jnp.where(adapter_pick, adapter_slot[None, :], 0), axis=1)


def adapter_delta(inputs, slot_ids, down_store, up_store):
    held_count = down_store.shape[0]
    model_width = down_store.shape[1]
    rank_size = down_store.shape[2]
    flat_down = jnp.transpose(down_store, (1, 0, 2)).reshape(model_width, held_count * rank_size)
    low_rank = jnp.dot(inputs, flat_down, preferred_element_type=jnp.float32)
    low_rank = low_rank.reshape(inputs.shape[0], held_count, rank_size)
    keep_mask = slot_ids[:, None] == jnp.arange(held_count, dtype=jnp.int32)[None, :]
    low_rank = jnp.where(keep_mask[:, :, None], low_rank, 0.0).astype(jnp.bfloat16)
    low_rank = low_rank.reshape(inputs.shape[0], held_count * rank_size)
    flat_up = up_store.reshape(held_count * rank_size, up_store.shape[2])
    return jnp.dot(low_rank, flat_up, preferred_element_type=jnp.float32)


def local(
    tokens,
    norm_gain,
    routes,
    route_gates,
    lengths,
    request_adapter,
    adapter_slot,
    expert_gate,
    expert_up,
    expert_down,
    shared_gate,
    shared_up_weight,
    shared_down,
    adapter_down,
    adapter_up,
    head_weight,
):
    tok_rows = tokens.shape[0]
    model_width = tokens.shape[1]
    route_count = routes.shape[1]
    tensor_size = lax.axis_size("tensor")
    tensor_pos = lax.axis_index("tensor")
    data_pos = lax.axis_index("dp")
    local_experts = expert_gate.shape[0]
    all_experts = local_experts * tensor_size
    slot_range = jnp.arange(CAP, dtype=jnp.int32)
    normed = apply_norm(tokens, norm_gain)
    numbers = jnp.arange(all_experts, dtype=jnp.int32)
    route_hits = routes[:, :, None] == numbers[None, None, :]
    chosen = jnp.any(route_hits, axis=1)
    weight = jnp.sum(
        jnp.where(route_hits, route_gates[:, :, None], jnp.zeros((), jnp.bfloat16)), axis=1
    )
    slot_place = jnp.cumsum(chosen.astype(jnp.int32), axis=0) - 1
    pooled, pooled_routes = (
        lax.all_gather(normed, "tensor", axis=0, tiled=True),
        lax.all_gather(routes.astype(jnp.bfloat16), "tensor", axis=0, tiled=True),
    )
    pooled = pooled.reshape(tensor_size, tok_rows, model_width)
    source_routes = pooled_routes.astype(jnp.int32).reshape(tensor_size, tok_rows, route_count)
    own_numbers = tensor_pos * local_experts + jnp.arange(local_experts, dtype=jnp.int32)
    source_hits = source_routes[:, :, :, None] == own_numbers[None, None, None, :]
    source_chosen = jnp.any(source_hits, axis=2)
    source_place = jnp.cumsum(source_chosen.astype(jnp.int32), axis=1) - 1
    source_pick = source_chosen[:, :, :, None] & (
        source_place[:, :, :, None] == slot_range[None, None, None, :]
    )
    source_pick = jnp.where(source_pick, 1.0, 0.0).astype(jnp.bfloat16)
    incoming = jnp.einsum(
        "sijc,sid->sjcd", source_pick, pooled, preferred_element_type=jnp.float32
    ).astype(jnp.bfloat16)
    gate_portion = jnp.einsum(
        "secd,edf->secf", incoming, expert_gate, preferred_element_type=jnp.float32
    )
    up_part = jnp.einsum("secd,edf->secf", incoming, expert_up, preferred_element_type=jnp.float32)
    hidden = (jax.nn.silu(gate_portion) * up_part).astype(jnp.bfloat16)
    expert_out = jnp.einsum(
        "secf,efd->secd", hidden, expert_down, preferred_element_type=jnp.float32
    ).astype(jnp.bfloat16)
    returned_rows = lax.all_to_all(expert_out, "tensor", split_axis=0, concat_axis=0, tiled=True)
    returned_rows = returned_rows.reshape(all_experts, CAP, model_width)
    mixing_result = jnp.where(
        slot_place[:, :, None] == slot_range[None, None, :],
        weight[:, :, None],
        jnp.zeros((), jnp.bfloat16),
    )
    routed_output = jnp.einsum(
        "kbt,btw->kw", mixing_result, returned_rows, preferred_element_type=jnp.float32
    )
    own_base = (data_pos * tensor_size + tensor_pos) * tok_rows
    own_positions = own_base + jnp.arange(tok_rows, dtype=jnp.int32)
    peer_rows = lax.all_gather(normed, "dp", axis=0, tiled=True)
    shared_sum = lax.psum_scatter(
        feed_forward(peer_rows, shared_gate, shared_up_weight, shared_down),
        "dp",
        scatter_dimension=0,
        tiled=True,
    )
    own_slots = token_slots(own_positions, lengths, request_adapter, adapter_slot)
    store_down, store_up = (
        lax.all_gather(adapter_down, "dp", axis=0, tiled=True),
        lax.all_gather(adapter_up, "dp", axis=0, tiled=True),
    )
    summed = routed_output + shared_sum + adapter_delta(normed, own_slots, store_down, store_up)
    sublayer_out = summed.astype(jnp.bfloat16)
    request_ends = jnp.cumsum(lengths)
    last_pick = jnp.where(request_ends[:, None] - 1 == own_positions[None, :], 1.0, 0.0).astype(
        jnp.bfloat16
    )
    last_part = jnp.dot(last_pick, sublayer_out, preferred_element_type=jnp.float32)
    last_states = lax.psum(last_part, ("dp", "tensor"))
    last_norm = jnp.sqrt(jnp.sum(last_states * last_states, axis=1))
    logits = jnp.dot(
        last_states.astype(jnp.bfloat16), head_weight, preferred_element_type=jnp.float32
    )
    block_logit = lax.pmax(jnp.max(logits, axis=1), "dp")
    return (sublayer_out, last_norm, block_logit[:, None])


def solution(mesh):
    placed = (
        P(("dp", "tensor"), None),
        P(),
        P(("dp", "tensor"), None),
        P(("dp", "tensor"), None),
        P(),
        P(),
        P(),
        P("tensor", None, None),
        P("tensor", None, None),
        P("tensor", None, None),
        P(None, "dp"),
        P(None, "dp"),
        P("dp", None),
        P("dp", None, None),
        P("dp", None, None),
        P(None, ("dp", "tensor")),
    )
    return jax.shard_map(
        local,
        mesh=mesh,
        in_specs=placed,
        out_specs=(P(("dp", "tensor"), None), P(), P(None, "tensor")),
        check_vma=False,
    )
```

profile of v0, /device:TPU:0, one launch (start us, length us, event | category | flops | bytes accessed | tf_op | source)
XLA Modules:
  0.0 401.9 jit_solution(9235097486257809376)
XLA Ops:
  7.2 0.9 convert_element_type.84
  8.1 1.3 fusion.41
  9.4 2.0 fusion.43
  11.5 0.7 all-gather.5.cloned.1.call-update
  12.3 32.6 %all-gather.7.cloned.1.call-done = bf16[512,2048]{1,0:T(8,128)(2,1)} async-done(((bf16[128,2048]{1,0:T(8,128)(2,1)}), bf16[512,2048]{1,0:T(8,128)(2,1)}) %all-gather.7.cloned.1.call-update) | async-done | bytes 2097168 | tf_op jit(solution)/shard_map/all_gather | solution.py:119
  44.9 3.8 fusion.82
  48.7 6.3 %fusion.32 = f32[512,2048]{1,0:T(8,128)} fusion(bf16[352,2048]{1,0:T(8,128)(2,1)S(1)} %copy-done.8, bf16[512,2048]{1,0:T(8,128)(2,1)} %all-gather.7.cloned.1.call-done, bf16[2048,352]{0,1:T(8,128)(2,1)} %param.27, f32[512,352]{0,1:T(8,128)} %fusion.82), kind=kOutput, calls=%fused_computation.29 | convolution fusion | flops 1477476352 | bytes 9895936 | tf_op jit(solution)/shard_map/dot_general | solution.py:19
  55.1 1.0 copy-done.4
  56.0 1.1 copy.47
  57.2 24.6 %all_gather.15 = bf16[4096,6]{0,1:T(8,128)(2,1)S(1)} all-gather(bf16[128,6]{0,1:T(8,128)(2,1)S(1)} %convert_element_type.79), channel_id=1, replica_groups=mesh['dp'=4,'tensor'=32] {'tensor'}, dimensions={0}, use_global_device_ids=true | all-gather | bytes 50688 | tf_op jit(solution)/shard_map/all_gather | solution.py:84
  81.8 0.3 reduce_window_sum.31
  82.1 38.3 %all-gather.5.cloned.1.call-done = bf16[4096,2048]{1,0:T(8,128)(2,1)} async-done(((bf16[128,2048]{1,0:T(8,128)(2,1)}), bf16[4096,2048]{1,0:T(8,128)(2,1)}) %all-gather.5.cloned.1.call-update) | async-done | bytes 16777232 | tf_op jit(solution)/shard_map/all_gather | solution.py:83
  120.4 8.1 %convolution_convert_fusion = bf16[32,32,2048]{2,1,0:T(8,128)(2,1)S(1)} fusion(bf16[32,128,2048]{2,1,0:T(8,128)(2,1)} %bitcast.109, s32[32,128]{1,0:T(8,128)S(1)} %broadcast_add_fusion.1, pred[32,128]{1,0:T(8,128)(4,1)S(1)} %bitcast.111), kind=kOutput, calls=%fused_computation.16 | convolution fusion | flops 539492352 | bytes 20992000 | tf_op jit(solution)/shard_map/sijc,sid->sjcd/dot_general | solution.py:96
  128.5 2.1 copy-done.1
  130.6 10.7 %fusion.3 = f32[32,32,1408]{2,1,0:T(8,128)} fusion(bf16[32,32,2048]{2,1,0:T(8,128)(2,1)S(1)} %convolution_convert_fusion, bf16[1,2048,1408]{2,1,0:T(8,128)(2,1)} %param.24), kind=kOutput, calls=%fused_computation.4 | convolution fusion | flops 5905580032 | bytes 15728640 | tf_op jit(solution)/shard_map/secd,edf->secf/dot_general | solution.py:102
  141.3 21.0 %convert_bitcast_fusion = bf16[32,1,32,2048]{3,2,1,0:T(8,128)(2,1)} fusion(bf16[1,1408,2048]{2,1,0:T(8,128)(2,1)} %param.25, f32[32,32,1408]{2,1,0:T(8,128)} %fusion.3, bf16[32,32,2048]{2,1,0:T(8,128)(2,1)} %copy-done.1, bf16[1,2048,1408]{2,1,0:T(8,128)(2,1)} %param.23), kind=kOutput, calls=%fused_computation.15 | convolution fusion | flops 11821907968 | bytes 25690112 | tf_op jit(solution)/shard_map/secf,efd->secd/dot_general | solution.py:104
  162.4 5.2 %all-to-all-start = ((bf16[32,1,32,2048]{3,2,1,0:T(8,128)(2,1)}), bf16[32,1,32,2048]{3,2,1,0:T(8,128)(2,1)}, u32[]{:S(2)}, u32[]{:S(2)}) async-start(bf16[32,1,32,2048]{3,2,1,0:T(8,128)(2,1)} %convert_bitcast_fusion), calls=%async_computation | async-start | bytes 8388608 | tf_op jit(solution)/shard_map/all_to_all | solution.py:107
  167.7 0.5 all-gather.9.cloned.1.call-update
  168.2 0.3 all-reduce.2.cloned.1.call-start
  168.5 0.1 copy.42
  168.6 0.2 reduce_window_sum.30
  169.0 0.1 reduce.2
  169.5 50.9 %all-to-all-done = bf16[32,1,32,2048]{3,2,1,0:T(8,128)(2,1)} async-done(((bf16[32,1,32,2048]{3,2,1,0:T(8,128)(2,1)}), bf16[32,1,32,2048]{3,2,1,0:T(8,128)(2,1)}, u32[]{:S(2)}, u32[]{:S(2)}) %all-to-all-start) | async-done | bytes 4194336 | tf_op jit(solution)/shard_map/all_to_all | solution.py:107
  220.4 4.3 %fusion.23 = f32[128,2048]{1,0:T(8,128)} fusion(f32[128,2048]{1,0:T(8,128)} %reduce-scatter.2.cloned.1.call-done, bf16[32,1,32,2048]{3,2,1,0:T(8,128)(2,1)} %all-to-all-done, s32[128,32]{0,1:T(8,128)S(1)} %copy.43, bf16[128,32]{0,1:T(8,128)(2,1)S(1)} %fusion.68), kind=kOutput, calls=%fused_computation.21 | convolution fusion | flops 537395200 | bytes 6316032 | tf_op jit(solution)/shard_map/kbt,btw->kw/dot_general | solution.py:114
  224.7 9.1 %all-gather.9.cloned.1.call-done = bf16[32,2048,16]{1,2,0:T(8,128)(2,1)} async-done(((bf16[8,2048,16]{1,2,0:T(8,128)(2,1)}), bf16[32,2048,16]{1,2,0:T(8,128)(2,1)}) %all-gather.9.cloned.1.call-update) | async-done | bytes 2097168 | tf_op jit(solution)/shard_map/all_gather | solution.py:128
  233.7 4.5 %fusion.26 = bf16[128,2048]{1,0:T(8,128)(2,1)S(1)} fusion(f32[128,2048]{1,0:T(8,128)} %fusion.23, bf16[32,16,2048]{2,0,1:T(8,128)(2,1)} %all-gather.11.cloned.1.call-done, bf16[32,16,2048]{2,1,0:T(8,128)(2,1)} %bitcast.110, bf16[128,2048]{1,0:T(8,128)(2,1)S(1)} %copy-done.2, pred[128,32]{0,1:T(8,128)(4,1)S(1)} %iota_compare_fusion.3), kind=kOutput, calls=%fused_computation.22 | convolution fusion | flops 537526272 | bytes 6295552 | tf_op jit(solution)/shard_map/dot_general | solution.py:44
  238.3 0.9 fusion.69
  239.2 143.1 %all-reduce.2.cloned.1.call-done = f32[24,2048]{1,0:T(8,128)} async-done(((f32[24,2048]{1,0:T(8,128)}), f32[24,2048]{1,0:T(8,128)}) %all-reduce.2.cloned.1.call-update) | async-done | bytes 196624 | tf_op jit(solution)/shard_map/psum | solution.py:138
  382.3 1.4 convolution_reduce_fusion
  383.7 9.7 %pmax.7 = f32[24,1]{0,1:T(1,128)} all-reduce(f32[24,1]{0,1:T(1,128)S(1)} %bitcast.112), channel_id=1, replica_groups=mesh['dp'=4,'tensor'=32] {'dp'}, use_global_device_ids=true, to_apply=%region_14.15 | all-reduce | flops 24 | bytes 192 | tf_op jit(solution)/shard_map/pmax | solution.py:143
  393.5 1.1 multiply_reduce_fusion
  394.6 0.5 sqrt.3
  (49 shorter events, 1.0 us)
Async XLA Ops:
  7.2 375.2 %copy-start = (bf16[2048,512]{1,0:T(8,128)(2,1)S(1)}, bf16[2048,512]{1,0:T(8,128)(2,1)}, u32[]{:S(2)}) copy-start(bf16[2048,512]{1,0:T(8,128)(2,1)} %param.31) | copy-start | bytes 6291460
  7.2 41.5 %copy-start.8 = (bf16[352,2048]{1,0:T(8,128)(2,1)S(1)}, bf16[352,2048]{1,0:T(8,128)(2,1)}, u32[]{:S(2)}) copy-start(bf16[352,2048]{1,0:T(8,128)(2,1)} %param.28) | copy-start | bytes 4325380
  7.2 37.7 %all-gather.7.cloned.1.call-start = ((), (), s32[]{:S(2)}) async-start(), calls=%async_computation.3 | async-start | bytes 2621440 | tf_op jit(solution)/shard_map/all_gather | solution.py:119
  11.5 109.0 %all-gather.5.cloned.1.call-start = ((), (), s32[]{:S(2)}) async-start(), calls=%async_computation.2 | async-start | bytes 17301504 | tf_op jit(solution)/shard_map/all_gather | solution.py:83
  12.2 157.3 %reduce-scatter.2.cloned.1.call-start = ((), (), s32[]{:S(2)}) async-start(), calls=%async_computation.4 | async-start | bytes 5242880 | tf_op jit(solution)/shard_map/reduce_scatter | solution.py:120
  55.0 1.0 copy-start.4
  55.0 2.1 copy-start.5
  55.0 169.6 %all-gather.11.cloned.1.call-start = ((), (), s32[]{:S(2)}) async-start(), calls=%async_computation.6 | async-start | bytes 2621440 | tf_op jit(solution)/shard_map/all_gather | solution.py:129
  128.5 2.1 copy-start.1
  162.3 6.5 %copy-start.7 = (s32[24]{0:T(128)S(1)}, s32[24]{0:T(128)}, u32[]{:S(2)}) copy-start(s32[24]{0:T(128)} %param.20) | copy-start | bytes 292
  162.3 6.9 %copy-start.9 = (s32[24]{0:T(128)S(1)}, s32[24]{0:T(128)}, u32[]{:S(2)}) copy-start(s32[24]{0:T(128)} %param.21) | copy-start | bytes 292
  162.3 7.0 %copy-start.10 = (s32[32]{0:T(128)S(1)}, s32[32]{0:T(128)}, u32[]{:S(2)}) copy-start(s32[32]{0:T(128)} %param.22) | copy-start | bytes 388
  162.4 7.1 %copy-start.6 = (bf16[128,6]{0,1:T(8,128)(2,1)S(1)}, bf16[128,6]{0,1:T(8,128)(2,1)}, u32[]{:S(2)}) copy-start(bf16[128,6]{0,1:T(8,128)(2,1)} %param.19) | copy-start | bytes 4612
  162.4 58.0 %all-to-all-start = ((bf16[32,1,32,2048]{3,2,1,0:T(8,128)(2,1)}), bf16[32,1,32,2048]{3,2,1,0:T(8,128)(2,1)}, u32[]{:S(2)}, u32[]{:S(2)}) async-start(bf16[32,1,32,2048]{3,2,1,0:T(8,128)(2,1)} %convert_bitcast_fusion), calls=%async_computation | async-start | bytes 8388608 | tf_op jit(solution)/shard_map/all_to_all | solution.py:107
  167.6 66.1 %copy-start.2 = (bf16[128,2048]{1,0:T(8,128)(2,1)S(1)}, bf16[128,2048]{1,0:T(8,128)(2,1)}, u32[]{:S(2)}) copy-start(bf16[128,2048]{1,0:T(8,128)(2,1)} %fusion.43) | copy-start | bytes 1572868
  167.6 66.1 %all-gather.9.cloned.1.call-start = ((), (), s32[]{:S(2)}) async-start(), calls=%async_computation.5 | async-start | bytes 2621440 | tf_op jit(solution)/shard_map/all_gather | solution.py:128
  168.2 214.1 %all-reduce.2.cloned.1.call-start = ((), (), s32[]{:S(2)}) async-start(), calls=%async_computation.7 | async-start | bytes 393216 | tf_op jit(solution)/shard_map/psum | solution.py:138
  238.3 156.8 %copy-start.3 = (bf16[128,2048]{1,0:T(8,128)(2,1)}, bf16[128,2048]{1,0:T(8,128)(2,1)S(1)}, u32[]{:S(2)}) copy-start(bf16[128,2048]{1,0:T(8,128)(2,1)S(1)} %fusion.26) | copy-start | bytes 1572868
Sparse Core Ops, SparseCore 0:
  11.6 33.2 all-gather.6
  47.7 72.6 all-gather.4
  122.8 46.1 reduce-scatter.1
  170.7 30.5 all-gather.10
  202.9 30.8 all-gather.8
  239.3 142.9 all-reduce.1
where the time goes:
time: 402 us
  waiting for transfers between devices  275 us (68%)
  matrix products  61.1 us (15%)
  blocking collectives  34.3 us (9%)
  between operations  14.3 us (4%)
  other arithmetic  6.28 us (2%)
  starting transfers between devices  5.69 us (1%)
  local copies, waits for them, and re-layouts  4.94 us (1%)
    psum x1, waiting for transfers between devices, local(): last_states = lax.psum(last_part, ('dp', 'tensor'))  143 us
    all_to_all x1, waiting for transfers between devices, local(): lax.all_to_all(expert_out, 'tensor', split_axis=0, concat_axis=0, tiled=T...  50.9 us
    all_gather x1, waiting for transfers between devices, local(): lax.all_gather(normed, 'tensor', axis=0, tiled=True)  38.3 us
    all_gather x1, waiting for transfers between devices, local(): peer_rows = lax.all_gather(normed, 'dp', axis=0, tiled=True)  32.6 us
    all_gather x1, blocking collectives, local(): lax.all_gather(routes.astype(jnp.bfloat16), 'tensor', axis=0, tiled=True)  24.6 us
    dot_general x1, matrix products, local(): jnp.einsum('secf,efd->secd', hidden, expert_down, preferred_element_type=...  21 us
    dot_general x1, matrix products, local(): jnp.einsum('secd,edf->secf', incoming, expert_up, preferred_element_type=...  10.7 us
    pmax x1, blocking collectives, local(): block_logit = lax.pmax(jnp.max(logits, axis=1), 'dp')  9.75 us
  transfers between devices with their start and end apart: 7, of which 5 were waited for; matrix products, arithmetic and copies ran while one was open for 14% of the time, Pallas kernels for 0%

commit v1 on v0

--- a/solution.py
+++ b/solution.py
@@ -2,6 +2,7 @@
 import jax.numpy as jnp
 from jax import lax
 from jax.sharding import PartitionSpec as P
+from jax.lax import psum
 
 CAP = 32
 
@@ -135,7 +136,7 @@
         jnp.bfloat16
     )
     last_part = jnp.dot(last_pick, sublayer_out, preferred_element_type=jnp.float32)
-    last_states = lax.psum(last_part, ("dp", "tensor"))
+    last_states = psum(psum(last_part, "tensor"), "dp")
     last_norm = jnp.sqrt(jnp.sum(last_states * last_states, axis=1))
     logits = jnp.dot(
         last_states.astype(jnp.bfloat16), head_weight, preferred_element_type=jnp.float32

time: 402 us -> 402 us (level)
    psum x1 -> x2, waiting for transfers between devices: 143 us -> 142 us  [local(): last_states = psum(psum(last_part, 'tensor'), 'dp')]
  transfers between devices with their start and end apart: 7 -> 8, of which waited for: 5 -> 6; matrix products, arithmetic and copies ran while one was open for 14% -> 14% of each run, Pallas kernels for 0% -> 0%
where the time goes in v1:
time: 402 us; the launch traced here: 401 us
  waiting for transfers between devices  275 us (68%)
  matrix products  61.1 us (15%)
  blocking collectives  34.4 us (9%)
  between operations  14.3 us (4%)
  other arithmetic  6.28 us (2%)
  starting transfers between devices  5.73 us (1%)
  local copies, waits for them, and re-layouts  4.94 us (1%)
    psum x2, waiting for transfers between devices, local(): last_states = psum(psum(last_part, 'tensor'), 'dp')  142 us
    all_to_all x1, waiting for transfers between devices, local(): lax.all_to_all(expert_out, 'tensor', split_axis=0, concat_axis=0, tiled=T...  50.9 us
    all_gather x1, waiting for transfers between devices, local(): lax.all_gather(normed, 'tensor', axis=0, tiled=True)  38.3 us
    all_gather x1, waiting for transfers between devices, local(): peer_rows = lax.all_gather(normed, 'dp', axis=0, tiled=True)  32.6 us
    all_gather x1, blocking collectives, local(): lax.all_gather(routes.astype(jnp.bfloat16), 'tensor', axis=0, tiled=True)  24.6 us
    dot_general x1, matrix products, local(): jnp.einsum('secf,efd->secd', hidden, expert_down, preferred_element_type=...  21 us
    dot_general x1, matrix products, local(): jnp.einsum('secd,edf->secf', incoming, expert_up, preferred_element_type=...  10.7 us
    pmax x1, blocking collectives, local(): block_logit = lax.pmax(jnp.max(logits, axis=1), 'dp')  9.85 us
  transfers between devices with their start and end apart: 8, of which 6 were waited for; matrix products, arithmetic and copies ran while one was open for 14% of the time, Pallas kernels for 0%

profile of v1, /device:TPU:0, one launch (start us, length us, event | category | flops | bytes accessed | tf_op | source)
XLA Modules:
  0.0 401.4 jit_solution(15870367274909506602)
XLA Ops:
  7.2 0.9 convert_element_type.84
  8.1 1.3 fusion.41
  9.4 2.0 fusion.43
  11.5 0.7 all-gather.5.cloned.1.call-update
  12.3 32.6 %all-gather.7.cloned.1.call-done = bf16[512,2048]{1,0:T(8,128)(2,1)} async-done(((bf16[128,2048]{1,0:T(8,128)(2,1)}), bf16[512,2048]{1,0:T(8,128)(2,1)}) %all-gather.7.cloned.1.call-update) | async-done | bytes 2097168 | tf_op jit(solution)/shard_map/all_gather | solution.py:120
  44.9 3.8 fusion.82
  48.7 6.3 %fusion.32 = f32[512,2048]{1,0:T(8,128)} fusion(bf16[352,2048]{1,0:T(8,128)(2,1)S(1)} %copy-done.8, bf16[512,2048]{1,0:T(8,128)(2,1)} %all-gather.7.cloned.1.call-done, bf16[2048,352]{0,1:T(8,128)(2,1)} %param.27, f32[512,352]{0,1:T(8,128)} %fusion.82), kind=kOutput, calls=%fused_computation.29 | convolution fusion | flops 1477476352 | bytes 9895936 | tf_op jit(solution)/shard_map/dot_general | solution.py:20
  55.1 1.0 copy-done.4
  56.0 1.1 copy.47
  57.2 24.6 %all_gather.15 = bf16[4096,6]{0,1:T(8,128)(2,1)S(1)} all-gather(bf16[128,6]{0,1:T(8,128)(2,1)S(1)} %convert_element_type.79), channel_id=1, replica_groups=mesh['dp'=4,'tensor'=32] {'tensor'}, dimensions={0}, use_global_device_ids=true | all-gather | bytes 50688 | tf_op jit(solution)/shard_map/all_gather | solution.py:85
  81.8 0.3 reduce_window_sum.31
  82.1 38.3 %all-gather.5.cloned.1.call-done = bf16[4096,2048]{1,0:T(8,128)(2,1)} async-done(((bf16[128,2048]{1,0:T(8,128)(2,1)}), bf16[4096,2048]{1,0:T(8,128)(2,1)}) %all-gather.5.cloned.1.call-update) | async-done | bytes 16777232 | tf_op jit(solution)/shard_map/all_gather | solution.py:84
  120.4 8.1 %convolution_convert_fusion = bf16[32,32,2048]{2,1,0:T(8,128)(2,1)S(1)} fusion(bf16[32,128,2048]{2,1,0:T(8,128)(2,1)} %bitcast.109, s32[32,128]{1,0:T(8,128)S(1)} %broadcast_add_fusion.1, pred[32,128]{1,0:T(8,128)(4,1)S(1)} %bitcast.111), kind=kOutput, calls=%fused_computation.16 | convolution fusion | flops 539492352 | bytes 20992000 | tf_op jit(solution)/shard_map/sijc,sid->sjcd/dot_general | solution.py:97
  128.5 2.1 copy-done.1
  130.6 10.7 %fusion.3 = f32[32,32,1408]{2,1,0:T(8,128)} fusion(bf16[32,32,2048]{2,1,0:T(8,128)(2,1)S(1)} %convolution_convert_fusion, bf16[1,2048,1408]{2,1,0:T(8,128)(2,1)} %param.24), kind=kOutput, calls=%fused_computation.4 | convolution fusion | flops 5905580032 | bytes 15728640 | tf_op jit(solution)/shard_map/secd,edf->secf/dot_general | solution.py:103
  141.3 21.0 %convert_bitcast_fusion = bf16[32,1,32,2048]{3,2,1,0:T(8,128)(2,1)} fusion(bf16[1,1408,2048]{2,1,0:T(8,128)(2,1)} %param.25, f32[32,32,1408]{2,1,0:T(8,128)} %fusion.3, bf16[32,32,2048]{2,1,0:T(8,128)(2,1)} %copy-done.1, bf16[1,2048,1408]{2,1,0:T(8,128)(2,1)} %param.23), kind=kOutput, calls=%fused_computation.15 | convolution fusion | flops 11821907968 | bytes 25690112 | tf_op jit(solution)/shard_map/secf,efd->secd/dot_general | solution.py:105
  162.4 5.2 %all-to-all-start = ((bf16[32,1,32,2048]{3,2,1,0:T(8,128)(2,1)}), bf16[32,1,32,2048]{3,2,1,0:T(8,128)(2,1)}, u32[]{:S(2)}, u32[]{:S(2)}) async-start(bf16[32,1,32,2048]{3,2,1,0:T(8,128)(2,1)} %convert_bitcast_fusion), calls=%async_computation | async-start | bytes 8388608 | tf_op jit(solution)/shard_map/all_to_all | solution.py:108
  167.7 0.5 all-gather.9.cloned.1.call-update
  168.2 0.3 all-reduce.3.cloned.1.call-start
  168.6 0.2 reduce_window_sum.30
  169.0 0.1 reduce.2
  169.5 50.9 %all-to-all-done = bf16[32,1,32,2048]{3,2,1,0:T(8,128)(2,1)} async-done(((bf16[32,1,32,2048]{3,2,1,0:T(8,128)(2,1)}), bf16[32,1,32,2048]{3,2,1,0:T(8,128)(2,1)}, u32[]{:S(2)}, u32[]{:S(2)}) %all-to-all-start) | async-done | bytes 4194336 | tf_op jit(solution)/shard_map/all_to_all | solution.py:108
  220.4 4.3 %fusion.23 = f32[128,2048]{1,0:T(8,128)} fusion(f32[128,2048]{1,0:T(8,128)} %reduce-scatter.2.cloned.1.call-done, bf16[32,1,32,2048]{3,2,1,0:T(8,128)(2,1)} %all-to-all-done, s32[128,32]{0,1:T(8,128)S(1)} %copy.43, bf16[128,32]{0,1:T(8,128)(2,1)S(1)} %fusion.68), kind=kOutput, calls=%fused_computation.21 | convolution fusion | flops 537395200 | bytes 6316032 | tf_op jit(solution)/shard_map/kbt,btw->kw/dot_general | solution.py:115
  224.7 9.1 %all-gather.9.cloned.1.call-done = bf16[32,2048,16]{1,2,0:T(8,128)(2,1)} async-done(((bf16[8,2048,16]{1,2,0:T(8,128)(2,1)}), bf16[32,2048,16]{1,2,0:T(8,128)(2,1)}) %all-gather.9.cloned.1.call-update) | async-done | bytes 2097168 | tf_op jit(solution)/shard_map/all_gather | solution.py:129
  233.7 4.5 %fusion.26 = bf16[128,2048]{1,0:T(8,128)(2,1)S(1)} fusion(f32[128,2048]{1,0:T(8,128)} %fusion.23, bf16[32,16,2048]{2,0,1:T(8,128)(2,1)} %all-gather.11.cloned.1.call-done, bf16[32,16,2048]{2,1,0:T(8,128)(2,1)} %bitcast.110, bf16[128,2048]{1,0:T(8,128)(2,1)S(1)} %copy-done.2, pred[128,32]{0,1:T(8,128)(4,1)S(1)} %iota_compare_fusion.3), kind=kOutput, calls=%fused_computation.22 | convolution fusion | flops 537526272 | bytes 6295552 | tf_op jit(solution)/shard_map/dot_general | solution.py:45
  238.3 0.9 fusion.69
  239.3 100.2 %all-reduce.3.cloned.1.call-done = f32[24,2048]{1,0:T(8,128)} async-done(((f32[24,2048]{1,0:T(8,128)}), f32[24,2048]{1,0:T(8,128)}) %all-reduce.3.cloned.1.call-update) | async-done | bytes 196624 | tf_op jit(solution)/shard_map/psum | solution.py:139
  339.4 42.3 %all-reduce.5.cloned.1.call-done = f32[24,2048]{1,0:T(8,128)} async-done(((f32[24,2048]{1,0:T(8,128)}), f32[24,2048]{1,0:T(8,128)}) %all-reduce.5.cloned.1.call-update) | async-done | bytes 196624 | tf_op jit(solution)/shard_map/psum | solution.py:139
  381.7 1.4 convolution_reduce_fusion
  383.2 9.8 %pmax.7 = f32[24,1]{0,1:T(1,128)} all-reduce(f32[24,1]{0,1:T(1,128)S(1)} %bitcast.112), channel_id=1, replica_groups=mesh['dp'=4,'tensor'=32] {'dp'}, use_global_device_ids=true, to_apply=%region_15.16 | all-reduce | flops 24 | bytes 192 | tf_op jit(solution)/shard_map/pmax | solution.py:144
  393.0 1.1 multiply_reduce_fusion
  394.1 0.5 sqrt.3
  (52 shorter events, 1.1 us)
Async XLA Ops:
  7.2 374.6 %copy-start = (bf16[2048,512]{1,0:T(8,128)(2,1)S(1)}, bf16[2048,512]{1,0:T(8,128)(2,1)}, u32[]{:S(2)}) copy-start(bf16[2048,512]{1,0:T(8,128)(2,1)} %param.31) | copy-start | bytes 6291460
  7.2 41.5 %copy-start.8 = (bf16[352,2048]{1,0:T(8,128)(2,1)S(1)}, bf16[352,2048]{1,0:T(8,128)(2,1)}, u32[]{:S(2)}) copy-start(bf16[352,2048]{1,0:T(8,128)(2,1)} %param.28) | copy-start | bytes 4325380
  7.2 37.7 %all-gather.7.cloned.1.call-start = ((), (), s32[]{:S(2)}) async-start(), calls=%async_computation.3 | async-start | bytes 2621440 | tf_op jit(solution)/shard_map/all_gather | solution.py:120
  11.5 109.0 %all-gather.5.cloned.1.call-start = ((), (), s32[]{:S(2)}) async-start(), calls=%async_computation.2 | async-start | bytes 17301504 | tf_op jit(solution)/shard_map/all_gather | solution.py:84
  12.2 157.3 %reduce-scatter.2.cloned.1.call-start = ((), (), s32[]{:S(2)}) async-start(), calls=%async_computation.4 | async-start | bytes 5242880 | tf_op jit(solution)/shard_map/reduce_scatter | solution.py:121
  55.0 1.0 copy-start.4
  55.0 2.1 copy-start.5
  55.0 169.6 %all-gather.11.cloned.1.call-start = ((), (), s32[]{:S(2)}) async-start(), calls=%async_computation.6 | async-start | bytes 2621440 | tf_op jit(solution)/shard_map/all_gather | solution.py:130
  128.5 2.1 copy-start.1
  162.3 6.5 %copy-start.7 = (s32[24]{0:T(128)S(1)}, s32[24]{0:T(128)}, u32[]{:S(2)}) copy-start(s32[24]{0:T(128)} %param.20) | copy-start | bytes 292
  162.3 6.9 %copy-start.9 = (s32[24]{0:T(128)S(1)}, s32[24]{0:T(128)}, u32[]{:S(2)}) copy-start(s32[24]{0:T(128)} %param.21) | copy-start | bytes 292
  162.3 7.0 %copy-start.10 = (s32[32]{0:T(128)S(1)}, s32[32]{0:T(128)}, u32[]{:S(2)}) copy-start(s32[32]{0:T(128)} %param.22) | copy-start | bytes 388
  162.4 7.1 %copy-start.6 = (bf16[128,6]{0,1:T(8,128)(2,1)S(1)}, bf16[128,6]{0,1:T(8,128)(2,1)}, u32[]{:S(2)}) copy-start(bf16[128,6]{0,1:T(8,128)(2,1)} %param.19) | copy-start | bytes 4612
  162.4 58.0 %all-to-all-start = ((bf16[32,1,32,2048]{3,2,1,0:T(8,128)(2,1)}), bf16[32,1,32,2048]{3,2,1,0:T(8,128)(2,1)}, u32[]{:S(2)}, u32[]{:S(2)}) async-start(bf16[32,1,32,2048]{3,2,1,0:T(8,128)(2,1)} %convert_bitcast_fusion), calls=%async_computation | async-start | bytes 8388608 | tf_op jit(solution)/shard_map/all_to_all | solution.py:108
  167.6 66.1 %copy-start.2 = (bf16[128,2048]{1,0:T(8,128)(2,1)S(1)}, bf16[128,2048]{1,0:T(8,128)(2,1)}, u32[]{:S(2)}) copy-start(bf16[128,2048]{1,0:T(8,128)(2,1)} %fusion.43) | copy-start | bytes 1572868
  167.6 66.1 %all-gather.9.cloned.1.call-start = ((), (), s32[]{:S(2)}) async-start(), calls=%async_computation.5 | async-start | bytes 2621440 | tf_op jit(solution)/shard_map/all_gather | solution.py:129
  168.2 171.2 %all-reduce.3.cloned.1.call-start = ((), (), s32[]{:S(2)}) async-start(), calls=%async_computation.7 | async-start | bytes 393216 | tf_op jit(solution)/shard_map/psum | solution.py:139
  238.3 156.3 %copy-start.3 = (bf16[128,2048]{1,0:T(8,128)(2,1)}, bf16[128,2048]{1,0:T(8,128)(2,1)S(1)}, u32[]{:S(2)}) copy-start(bf16[128,2048]{1,0:T(8,128)(2,1)S(1)} %fusion.26) | copy-start | bytes 1572868
  239.2 142.5 %all-reduce.5.cloned.1.call-start = ((), (), s32[]{:S(2)}) async-start(), calls=%async_computation.8 | async-start | bytes 393216 | tf_op jit(solution)/shard_map/psum | solution.py:139
Sparse Core Ops, SparseCore 0:
  11.6 33.2 all-gather.6
  47.7 72.6 all-gather.4
  122.8 46.1 reduce-scatter.1
  170.7 30.5 all-gather.10
  202.9 30.8 all-gather.8
  239.3 100.0 all-reduce.2
  341.7 39.9 all-reduce.4
